TPU v7x, 32 devices: a whole 2x2x4 slice. The times are simulated.
32 devices in a mesh: slab: 8 (over y, x, core), grp: 4 (over z).
Axes of the slice: x: 2, y: 2, z: 4, core: 2. Of those that a mesh axis runs over, the one named last changes fastest.
Arguments:
- resid7: float32 [512, 4096], P(None, ('slab', 'grp')), may hold values from -6 to 6
- interp73: float32 [8, 4], replicated, may hold values from -2 to 2
- interp31: float32 [4, 2], replicated, may hold values from -4 to 4
- elem_ops: float32 [8, 8, 4096], P(None, None, 'slab'), as said below
- conn: int32 [8, 4096], P(None, 'slab'), may hold values from 0 to 1121, as said below
- faces: int32 [2, 8, 561], P(None, 'slab'), may hold values from 0 to 1121, as said below
Outputs:
- correction3: float32 [64, 4096], P(None, ('slab', 'grp'))
Inputs may be any that keep to these rules, and one draw needn't show every extreme that they name: `conn`: the 512 columns of a slab describe a block of 32 x 16 x 1 hexahedra stacked along the long direction; column e lists the corners of one element, the corner at offsets (i, j, k) along (long, second, first direction) in row 4 i + 2 j + k; the slab's nodes are numbered 0 to 1121 in some order and every one of them is a corner of some element. faces[0, s] lists the 561 nodes of slab s on its face toward slab s - 1, faces[1, s] those on its face toward slab s + 1, all distinct; faces[1, s, f] and faces[0, s + 1, f] are the same point of the mesh. `elem_ops`: each element's matrix is symmetric, and each diagonal entry is positive and larger than the sum of magnitudes of the other entries of its row.
All inputs are finite; a program needn't handle non-finite values.
Results may differ from a plain program's by a relative error of at most 0.0003.
Values sent between devices are 32-bit elements; how exact they have to be, the bound alone decides.
A program may use at most 64 MiB of HBM per device.

v0:
```python
import jax
import jax.numpy as jnp
from jax import lax
from jax.sharding import PartitionSpec as P

EX = 32
EY = 16
SWEEPS = 2


lam_low = 0.3
lam_high = 1.9


def extended(array, sides, width):
    for axis, dim in sides:
        count, length = (lax.axis_size(axis), array.shape[dim])
        up = [(i, (i + 1) % count) for i in range(count - 1)]
        down = [(j, i) for i, j in up]
        last = lax.slice_in_dim(array, length - width, length, axis=dim)
        first = lax.slice_in_dim(array, 0, width, axis=dim)
        before = lax.ppermute(last, axis, up)
        after = lax.ppermute(first, axis, down)
        array = jnp.concatenate([before, array, after], axis=dim)
    return array


def restrict_high(block, interp73):
    hi = lax.Precision.HIGHEST
    width = block.shape[1]
    cube = block.reshape(8, 8, 8, width)
    cube = jnp.einsum("kc,ijkm->ijcm", interp73, cube, precision=hi)
    cube = jnp.einsum("jb,ijcm->ibcm", interp73, cube, precision=hi)
    cube = jnp.einsum("ia,ibcm->abcm", interp73, cube, precision=hi)
    return cube.reshape(64, width)


def restrict_low(block, interp31):
    hi = lax.Precision.HIGHEST
    width = block.shape[1]
    cube = block.reshape(4, 4, 4, width)
    cube = jnp.einsum("kc,ijkm->ijcm", interp31, cube, precision=hi)
    cube = jnp.einsum("jb,ijcm->ibcm", interp31, cube, precision=hi)
    cube = jnp.einsum("ia,ibcm->abcm", interp31, cube, precision=hi)
    return cube.reshape(8, width)


def prolong(coarse, interp31):
    hi = lax.Precision.HIGHEST
    width = coarse.shape[1]
    cube = coarse.reshape(2, 2, 2, width)
    cube = jnp.einsum("ck,ijkm->ijcm", interp31, cube, precision=hi)
    cube = jnp.einsum("bj,ijcm->ibcm", interp31, cube, precision=hi)
    cube = jnp.einsum("ai,ibcm->abcm", interp31, cube, precision=hi)
    return cube.reshape(64, width)


def assemble(values, conn_ids, count):
    layers = values.shape[0]
    flat = values.reshape(layers, -1).T
    summed = jax.ops.segment_sum(flat, conn_ids.reshape(-1), num_segments=count)
    return summed.T


def element_term(operators, conn_ids, field):
    return jnp.einsum("pqe,qe->pe", operators, field[conn_ids], precision=lax.Precision.HIGHEST)


def share(nodes, faces):
    lower = faces[0, 0]
    upper = faces[1, 0]
    planes = jnp.stack([nodes[:, lower], nodes[:, upper]], axis=1)
    padded = extended(planes, (("slab", 1),), 1)
    return nodes.at[:, lower].add(padded[:, 0]).at[:, upper].add(padded[:, 3])


def local(resid7, interp73, interp31, elem_ops, conn, faces):
    own = resid7.shape[1]
    slab_elems = conn.shape[1]
    layers = slab_elems // (EX * EY)
    count = (EX + 1) * (EY + 1) * (layers + 1)
    start = lax.axis_index("grp") * own
    own_conn = lax.dynamic_slice_in_dim(conn, start, own, 1)
    middle_res = restrict_high(resid7, interp73)
    blocks = lax.all_gather(middle_res, "grp", axis=1, tiled=True)
    slab_res = restrict_low(blocks, interp31)
    pair = jnp.stack([slab_res, jnp.einsum("ppe->pe", elem_ops)])
    both_nodes = assemble(pair, conn, count)
    shared = share(both_nodes, faces)
    rhs = shared[0]
    diag = shared[1]
    theta = 0.5 * (lam_high + lam_low)
    delta = 0.5 * (lam_high - lam_low)
    sigma = theta / delta
    inverse = 1.0 / diag
    direction = inverse * rhs / theta
    solution = direction
    remain = rhs
    rho = 1.0 / sigma
    for sweep in range(SWEEPS):
        nodes = assemble(element_term(elem_ops, conn, direction)[None], conn, count)
        remain = remain - share(nodes, faces)[0]
        rho_new = 1.0 / (2.0 * sigma - rho)
        direction = rho_new * rho * direction + 2.0 * rho_new / delta * inverse * remain
        solution = solution + direction
        rho = rho_new
    return prolong(solution[own_conn], interp31)


def solution(mesh):
    in_specs = (
        P(None, ("slab", "grp")),
        P(),
        P(),
        P(None, None, "slab"),
        P(None, "slab"),
        P(None, "slab", None),
    )
    out_specs = P(None, ("slab", "grp"))
    return jax.shard_map(local, mesh=mesh, in_specs=in_specs, out_specs=out_specs, check_vma=False)
```

profile of v0, /device:TPU:0, one launch (start us, length us, event | category | flops | bytes accessed | tf_op | source)
XLA Modules:
  0.0 220.1 jit_solution(7532873134520829746)
XLA Ops:
  4.7 15.1 %all_gather.3 = f32[64,512]{1,0:T(8,128)S(1)} all-gather(f32[64,128]{1,0:T(8,128)S(1)} %bitcast.100), channel_id=1, replica_groups=mesh['slab'=8,'grp'=4] {'grp'}, dimensions={1}, use_global_device_ids=true | all-gather | bytes 163840 | tf_op jit(solution)/shard_map/all_gather | solution.py:85
  23.5 22.5 %scatter_custom_fusion = f32[1122,2]{1,0:T(8,128)S(1)} fusion(s32[4096]{0:T(1024)S(1)} %bitcast.109, f32[4096,2]{1,0:T(8,128)S(1)} %copy.46, f32[]{:T(128)} %constant.13.clone.1), kind=kCustom, calls=%fused_computation.31 | custom fusion | flops 8192 | bytes 8980 | tf_op jit(solution)/shard_map/scatter-add | solution.py:61
  45.9 1.6 gather_fusion
  47.6 1.3 collective-permute-start
  48.9 1.6 gather_fusion.1
  50.5 1.3 collective-permute-start.1
  51.9 6.4 %scatter_custom_fusion.1 = f32[2,1122]{0,1:T(8,128)S(1)} fusion(f32[2,1122]{0,1:T(8,128)S(1)} %bitcast.99, s32[561]{0:T(1024)S(1)} %get-tuple-element.6, f32[2,1,561]{0,2,1:T(8,128)S(1)} %collective-permute-done), kind=kCustom, calls=%fused_computation.29 | custom fusion | flops 1122 | bytes 299792 | tf_op jit(solution)/shard_map/scatter-add | solution.py:74
  58.3 6.4 %scatter_custom_fusion.2 = f32[2,1122]{0,1:T(8,128)S(1)} fusion(f32[2,1122]{0,1:T(8,128)S(1)} %scatter_custom_fusion.1, s32[561]{0:T(1024)S(1)} %get-tuple-element.5, f32[2,1,561]{0,2,1:T(8,128)S(1)} %collective-permute-done.1), kind=kCustom, calls=%fused_computation.27 | custom fusion | flops 1122 | bytes 299792 | tf_op jit(solution)/shard_map/scatter-add | solution.py:74
  65.4 23.0 %gather_fusion.2 = f32[4096]{0:T(1024)S(1)} fusion(f32[1122]{0:T(1024)S(1)} %get-tuple-element.7, s32[4096]{0:T(1024)S(1)} %broadcast_clamp_fusion), kind=kCustom, calls=%fused_computation.2 | custom fusion | bytes 49152 | tf_op jit(solution)/shard_map/gather | solution.py:66
  88.5 26.6 %scatter_custom_fusion.3 = f32[1122]{0:T(1024)S(1)} fusion(s32[4096]{0:T(1024)S(1)} %bitcast.110, f32[4096]{0:T(1024)S(1)} %bitcast.113, f32[]{:T(128)} %constant.13.clone.1), kind=kCustom, calls=%fused_computation.62 | custom fusion | flops 4096 | bytes 4492 | tf_op jit(solution)/shard_map/scatter-add | solution.py:61
  115.1 3.6 %gather_fusion.3 = f32[561]{0:T(1024)S(1)} fusion(f32[1122]{0:T(1024)S(1)} %scatter_custom_fusion.3, s32[1024]{0:T(1024)S(1)} %get-tuple-element.12), kind=kCustom, calls=%fused_computation.3 | custom fusion | bytes 6732 | tf_op jit(solution)/shard_map/gather | solution.py:72
  118.7 4.7 %collective-permute-start.2 = (f32[1,1,561]{2,1,0:T(1,128)S(1)}, f32[1,1,561]{2,1,0:T(1,128)S(1)}, u32[]{:S(2)}, u32[]{:S(2)}) collective-permute-start(f32[1,1,561]{2,1,0:T(1,128)S(1)} %stack.31), channel_id=1, source_target_pairs={{0,4},{4,8},{8,12},{12,16},{16,20},{20,24},{24,28},{1,5},{5,9},{9,... | collective-permute-start | bytes 6740 | tf_op jit(solution)/shard_map/ppermute | solution.py:22
  123.4 3.6 %gather_fusion.4 = f32[561]{0:T(1024)S(1)} fusion(f32[1122]{0:T(1024)S(1)} %scatter_custom_fusion.3, s32[1024]{0:T(1024)S(1)} %get-tuple-element.11), kind=kCustom, calls=%fused_computation.4 | custom fusion | bytes 6732 | tf_op jit(solution)/shard_map/gather | solution.py:72
  127.0 1.3 collective-permute-start.3
  128.3 5.2 %scatter_fusion = f32[1122]{0:T(1024)S(1)} fusion(f32[1122]{0:T(1024)S(1)} %scatter_custom_fusion.3, s32[561]{0:T(1024)S(1)} %get-tuple-element.6, f32[561]{0:T(1024)S(1)} %reduce.5), kind=kCustom, calls=%fused_computation.13 | custom fusion | flops 561 | bytes 8976 | tf_op jit(solution)/shard_map/scatter-add | solution.py:74
  133.6 5.2 %scatter_fusion.1 = f32[1122]{0:T(1024)S(1)} fusion(f32[1122]{0:T(1024)S(1)} %scatter_fusion, s32[561]{0:T(1024)S(1)} %get-tuple-element.5, f32[561]{0:T(1024)S(1)} %reduce.6), kind=kCustom, calls=%fused_computation.14 | custom fusion | flops 561 | bytes 8976 | tf_op jit(solution)/shard_map/scatter-add | solution.py:74
  138.8 23.0 %gather_fusion.5 = f32[4096]{0:T(1024)S(1)} fusion(f32[1122]{0:T(1024)S(1)} %add_reduce_fusion, s32[4096]{0:T(1024)S(1)} %broadcast_clamp_fusion), kind=kCustom, calls=%fused_computation.5 | custom fusion | bytes 49152 | tf_op jit(solution)/shard_map/gather | solution.py:66
  162.0 26.6 %scatter_custom_fusion.6 = f32[1122]{0:T(1024)S(1)} fusion(s32[4096]{0:T(1024)S(1)} %bitcast.111, f32[4096]{0:T(1024)S(1)} %bitcast.112, f32[]{:T(128)} %constant.13.clone.1), kind=kCustom, calls=%fused_computation.60 | custom fusion | flops 4096 | bytes 4492 | tf_op jit(solution)/shard_map/scatter-add | solution.py:61
  188.5 3.6 %gather_fusion.7 = f32[561]{0:T(1024)S(1)} fusion(f32[1122]{0:T(1024)S(1)} %scatter_custom_fusion.6, s32[1024]{0:T(1024)S(1)} %get-tuple-element.11), kind=kCustom, calls=%fused_computation.7 | custom fusion | bytes 6732 | tf_op jit(solution)/shard_map/gather | solution.py:72
  192.1 3.6 %gather_fusion.6 = f32[561]{0:T(1024)S(1)} fusion(f32[1122]{0:T(1024)S(1)} %scatter_custom_fusion.6, s32[1024]{0:T(1024)S(1)} %get-tuple-element.12), kind=kCustom, calls=%fused_computation.6 | custom fusion | bytes 6732 | tf_op jit(solution)/shard_map/gather | solution.py:72
  195.7 5.0 %collective-permute-start.4 = (f32[1,1,561]{2,1,0:T(1,128)S(1)}, f32[1,1,561]{2,1,0:T(1,128)S(1)}, u32[]{:S(2)}, u32[]{:S(2)}) collective-permute-start(f32[1,1,561]{2,1,0:T(1,128)S(1)} %stack.33), channel_id=1, source_target_pairs={{0,4},{4,8},{8,12},{12,16},{16,20},{20,24},{24,28},{1,5},{5,9},{9,... | collective-permute-start | bytes 6740 | tf_op jit(solution)/shard_map/ppermute | solution.py:22
  202.1 5.2 %scatter_fusion.2 = f32[1122]{0:T(1024)S(1)} fusion(f32[1122]{0:T(1024)S(1)} %scatter_custom_fusion.6, s32[561]{0:T(1024)S(1)} %get-tuple-element.6, f32[561]{0:T(1024)S(1)} %reduce.8), kind=kCustom, calls=%fused_computation.16 | custom fusion | flops 561 | bytes 8976 | tf_op jit(solution)/shard_map/scatter-add | solution.py:74
  207.3 5.2 %scatter_fusion.3 = f32[1122]{0:T(1024)S(1)} fusion(f32[1122]{0:T(1024)S(1)} %scatter_fusion.2, s32[561]{0:T(1024)S(1)} %get-tuple-element.5, f32[561]{0:T(1024)S(1)} %reduce.9), kind=kCustom, calls=%fused_computation.17 | custom fusion | flops 561 | bytes 8976 | tf_op jit(solution)/shard_map/scatter-add | solution.py:74
  212.6 6.2 %gather_fusion.8 = f32[1024]{0:T(1024)S(1)} fusion(f32[1122]{0:T(1024)S(1)} %add_add_fusion, s32[1024]{0:T(1024)S(1)} %fusion.16), kind=kCustom, calls=%fused_computation.8 | custom fusion | bytes 12288 | tf_op jit(solution)/shard_map/gather | solution.py:107
  (64 shorter events, 11.9 us)
Async XLA Ops:
  0.0 1.8 copy-start
  0.0 23.4 %copy-start.4 = (s32[2,1,561]{2,1,0:T(1,128)S(1)}, s32[2,1,561]{2,1,0:T(1,128)}, u32[]{:S(2)}) copy-start(s32[2,1,561]{2,1,0:T(1,128)} %param.11) | copy-start | bytes 13468
  2.8 49.0 %copy-start.2 = (s32[8,512]{1,0:T(8,128)S(1)}, s32[8,512]{1,0:T(8,128)}, u32[]{:S(2)}) copy-start(s32[8,512]{1,0:T(8,128)} %param.10) | copy-start | bytes 49156
  47.6 4.3 %collective-permute-start = (f32[2,1,561]{0,2,1:T(8,128)S(1)}, f32[2,1,561]{0,2,1:T(8,128)S(1)}, u32[]{:S(2)}, u32[]{:S(2)}) collective-permute-start(f32[2,1,561]{0,2,1:T(8,128)S(1)} %bitcast.116), channel_id=1, source_target_pairs={{0,4},{4,8},{8,12},{12,16},{16,20},{20,24},{24,28},{1,5},{5,9},{9,... | collective-permute-start | bytes 13472 | tf_op jit(solution)/shard_map/ppermute | solution.py:22
  50.5 7.8 %collective-permute-start.1 = (f32[2,1,561]{0,2,1:T(8,128)S(1)}, f32[2,1,561]{0,2,1:T(8,128)S(1)}, u32[]{:S(2)}, u32[]{:S(2)}) collective-permute-start(f32[2,1,561]{0,2,1:T(8,128)S(1)} %bitcast.115), channel_id=1, source_target_pairs={{4,0},{8,4},{12,8},{16,12},{20,16},{24,20},{28,24},{5,1},{9,5},{13... | collective-permute-start | bytes 13472 | tf_op jit(solution)/shard_map/ppermute | solution.py:23
  65.4 23.1 %copy-start.1 = (f32[8,8,512]{2,1,0:T(8,128)S(1)}, f32[8,8,512]{2,1,0:T(8,128)}, u32[]{:S(2)}) copy-start(f32[8,8,512]{2,1,0:T(8,128)} %param.9) | copy-start | bytes 393220
  118.7 9.6 %collective-permute-start.2 = (f32[1,1,561]{2,1,0:T(1,128)S(1)}, f32[1,1,561]{2,1,0:T(1,128)S(1)}, u32[]{:S(2)}, u32[]{:S(2)}) collective-permute-start(f32[1,1,561]{2,1,0:T(1,128)S(1)} %stack.31), channel_id=1, source_target_pairs={{0,4},{4,8},{8,12},{12,16},{16,20},{20,24},{24,28},{1,5},{5,9},{9,... | collective-permute-start | bytes 6740 | tf_op jit(solution)/shard_map/ppermute | solution.py:22
  127.0 6.6 %collective-permute-start.3 = (f32[1,1,561]{2,1,0:T(1,128)S(1)}, f32[1,1,561]{2,1,0:T(1,128)S(1)}, u32[]{:S(2)}, u32[]{:S(2)}) collective-permute-start(f32[1,1,561]{2,1,0:T(1,128)S(1)} %stack.32), channel_id=1, source_target_pairs={{4,0},{8,4},{12,8},{16,12},{20,16},{24,20},{28,24},{5,1},{9,5},{13... | collective-permute-start | bytes 6740 | tf_op jit(solution)/shard_map/ppermute | solution.py:23
  195.7 6.4 %collective-permute-start.4 = (f32[1,1,561]{2,1,0:T(1,128)S(1)}, f32[1,1,561]{2,1,0:T(1,128)S(1)}, u32[]{:S(2)}, u32[]{:S(2)}) collective-permute-start(f32[1,1,561]{2,1,0:T(1,128)S(1)} %stack.33), channel_id=1, source_target_pairs={{0,4},{4,8},{8,12},{12,16},{16,20},{20,24},{24,28},{1,5},{5,9},{9,... | collective-permute-start | bytes 6740 | tf_op jit(solution)/shard_map/ppermute | solution.py:22
  200.7 6.6 %collective-permute-start.5 = (f32[1,1,561]{2,1,0:T(1,128)S(1)}, f32[1,1,561]{2,1,0:T(1,128)S(1)}, u32[]{:S(2)}, u32[]{:S(2)}) collective-permute-start(f32[1,1,561]{2,1,0:T(1,128)S(1)} %stack.34), channel_id=1, source_target_pairs={{4,0},{8,4},{12,8},{16,12},{20,16},{24,20},{28,24},{5,1},{9,5},{13... | collective-permute-start | bytes 6740 | tf_op jit(solution)/shard_map/ppermute | solution.py:23
  212.6 6.2 %copy-start.3 = (f32[4,2]{0,1:T(2,128)S(1)}, f32[4,2]{0,1:T(2,128)}, u32[]{:S(2)}) copy-start(f32[4,2]{0,1:T(2,128)} %param.8) | copy-start | bytes 100
where the time goes:
time: 225 us; the launch traced here: 220 us
  other arithmetic  111 us (49%)
  local copies, waits for them, and re-layouts  72.5 us (32%)
  blocking collectives  15.1 us (7%)
  starting transfers between devices  14.9 us (7%)
  matrix products  6.36 us (3%)
    scatter-add x3, other arithmetic, assemble(): summed = jax.ops.segment_sum(flat, conn_ids.reshape(-1), num_segments=count)  75.6 us
    gather x4, local copies, waits for them, and re-layouts, element_term(): field[conn_ids]  46.1 us
    scatter-add x6, other arithmetic, share(): return nodes.at[:, lower].add(padded[:, 0]).at[:, upper].add(padded[:, 3])  33.7 us
    gather x6, local copies, waits for them, and re-layouts, share(): planes = jnp.stack([nodes[:, lower], nodes[:, upper]], axis=1)  17.5 us
    all_gather x1, blocking collectives, local(): blocks = lax.all_gather(middle_res, 'grp', axis=1, tiled=True)  15.1 us
    ppermute x3, starting transfers between devices, extended(): before = lax.ppermute(last, axis, up)  11 us
    gather x1, local copies, waits for them, and re-layouts, local(): return prolong(solution[own_conn], interp31)  6.15 us
  transfers between devices with their start and end apart: 6, of which 0 were waited for; matrix products, arithmetic and copies ran while one was open for 10% of the time, Pallas kernels for 0%

commit v1 on v0

--- a/solution.py
+++ b/solution.py
@@ -1,6 +1,10 @@
+import functools
+
 import jax
 import jax.numpy as jnp
 from jax import lax
+from jax.experimental import pallas as pl
+from jax.experimental.pallas import tpu as pltpu
 from jax.sharding import PartitionSpec as P
 
 EX = 32
@@ -107,6 +111,339 @@
     return prolong(solution[own_conn], interp31)
 
 
+STRIDE = EX + 1
+POINTS = (EX + 1) * (EY + 1)
+LANES = (POINTS + 127) // 128 * 128
+LINE = EX * EY
+BLOCKS = LINE // 128
+MESH = pl.DeviceIdType.MESH
+VMEM = pl.BlockSpec(memory_space=pltpu.VMEM)
+SMEM = pl.BlockSpec(memory_space=pltpu.SMEM)
+
+
+def rows_of(shape):
+    return lax.broadcasted_iota(jnp.int32, shape, 0)
+
+
+def spread(row, count=8):
+    return jnp.broadcast_to(row, (count, row.shape[1]))
+
+
+def stack_rows(rows):
+    sub = rows_of((8, rows[0].shape[1]))
+    out = spread(rows[0])
+    for at in range(1, 8):
+        out = jnp.where(sub == at, spread(rows[at]), out)
+    return out
+
+
+def parts_of(value):
+    hi = value.astype(jnp.bfloat16).astype(jnp.float32)
+    left = value - hi
+    mid = left.astype(jnp.bfloat16).astype(jnp.float32)
+    return jnp.concatenate([hi, mid, left - mid], axis=0).astype(jnp.bfloat16)
+
+
+def join_parts(value):
+    third = value.shape[0] // 3
+    return value[:third] + value[third : 2 * third] + value[2 * third :]
+
+
+def gather_sums(corners):
+    sub = rows_of(corners.shape)
+    odd, second = (sub % 2 == 1, sub // 2 % 2 == 1)
+    part = jnp.where(odd, pltpu.roll(corners, 1, 1), corners)
+    part = part + jnp.where(odd, pltpu.roll(part, 1, 0), pltpu.roll(part, 7, 0))
+    part = jnp.where(second, pltpu.roll(part, STRIDE, 1), part)
+    return part + jnp.where(second, pltpu.roll(part, 2, 0), pltpu.roll(part, 6, 0))
+
+
+def corner_values(nodes):
+    sub = rows_of(nodes.shape)
+    part = jnp.where(sub // 2 % 2 == 1, pltpu.roll(nodes, LANES - STRIDE, 1), nodes)
+    return jnp.where(sub % 2 == 1, pltpu.roll(part, LANES - 1, 1), part)
+
+
+def before(ids, mine, theirs):
+    column = jnp.broadcast_to(ids[theirs : theirs + 1], (128, LINE)).T
+    row = spread(ids[mine : mine + 1])
+    place = rows_of((8, LINE)).astype(jnp.float32)
+    total = jnp.zeros((8, LINE), jnp.float32)
+    for at in range(LINE // 8):
+        one = column[8 * at : 8 * at + 8]
+        same = jnp.concatenate([one] * BLOCKS, axis=1) == row
+        total = total + jnp.where(same, place + (8.0 * at + 1.0), 0.0)
+    return jnp.sum(total, axis=0, keepdims=True)
+
+
+def positions(conn):
+    ids = conn.astype(jnp.float32)
+    own = lax.broadcasted_iota(jnp.int32, (1, LINE), 1)
+    rows = []
+    for theirs in (1, 2):
+        found = before(ids, 0, theirs).astype(jnp.int32)
+        packed = jnp.where(found > 0, found - 1 + LINE, own)
+        rows += [packed[:, 128 * b : 128 * b + 128] for b in range(BLOCKS)]
+    state = stack_rows(rows)
+    sub = rows_of((8, 128))
+    for _ in range((EX - 1).bit_length()):
+        target = state % LINE
+        lane, block = (target % 128, target // 128)
+        got = jnp.zeros((8, 128), jnp.int32)
+        for b in range(BLOCKS):
+            table = jnp.where(sub < BLOCKS, spread(state[b : b + 1]), spread(state[BLOCKS + b : BLOCKS + b + 1]))
+            got = jnp.where(block == b, jnp.take_along_axis(table, lane, axis=1), got)
+        state = got + (state - target)
+    steps = state // LINE
+    return steps + STRIDE * pltpu.roll(steps, 4, 0)
+
+
+def one_hot(row):
+    return jnp.where(rows_of((LANES, row.shape[1])) == spread(row, LANES), 1.0, 0.0).astype(jnp.bfloat16)
+
+
+def setup_kernel(conn_ref, ops_ref, res_ref, table_ref, i73_ref, i31_ref, lex_ref, send_ref, pos_ref):
+    group = lax.axis_index("grp")
+    coef = [[sum(i73_ref[i, m] * i31_ref[m, a] for m in range(4)) for a in range(2)] for i in range(8)]
+    place = positions(conn_ref[...])
+
+    along_j = [[None] * 8, [None] * 8]
+    for j in range(8):
+        for a in range(2):
+            along_j[a][j] = sum(coef[i][a] * res_ref[64 * i + 8 * j : 64 * i + 8 * j + 8, :] for i in range(8))
+    last = [sum(table_ref[:, m : m + 1] * i31_ref[m, c] for m in range(4)) for c in range(2)]
+    rows = []
+    for a in range(2):
+        for b in range(2):
+            line = sum(coef[j][b] * along_j[a][j] for j in range(8))
+            for c in range(2):
+                rows.append(jnp.sum(last[c] * line, axis=0, keepdims=True))
+    low_res = stack_rows(rows)
+    lanes = pl.ds(pl.multiple_of(group * 128, 128), 128)
+    diagonal = stack_rows([ops_ref[p, p : p + 1, lanes] for p in range(8)])
+
+    mine = spread(place[0:1])
+    for b in range(1, BLOCKS):
+        mine = jnp.where(group == b, spread(place[b : b + 1]), mine)
+    pos_ref[...] = mine[0:1]
+    own_hot = one_hot(mine[0:1])
+    both = parts_of(jnp.concatenate([low_res, diagonal], axis=0))
+    both = join_parts(lax.dot_general(both, own_hot, (((1,), (1,)), ((), ())), preferred_element_type=jnp.float32))
+    for at in range(2):
+        nodes = gather_sums(both[8 * at : 8 * at + 8])
+        for plane in range(2):
+            send_ref[plane, at : at + 1, :] = nodes[4 * plane : 4 * plane + 1]
+
+    hot = jnp.concatenate([one_hot(place[b : b + 1]) for b in range(BLOCKS)], axis=1)
+    ops = parts_of(ops_ref[...].reshape(64, LINE))
+    lex = lax.dot_general(ops, hot, (((1,), (1,)), ((), ())), preferred_element_type=jnp.float32)
+    lex_ref[...] = join_parts(lex).reshape(8, 8, LANES)
+
+
+def smooth_kernel(slabs, groups, send_ref, lex_ref, pos_ref, table_ref, i31_ref, out_ref, got_own, got_side, out_side, in_side, own_send, own_recv, side_send, side_recv, face_send, face_recv):
+    slab, group = (lax.axis_index("slab"), lax.axis_index("grp"))
+    down, up = (lax.rem(slab + slabs - 1, slabs), lax.rem(slab + 1, slabs))
+    has = (slab > 0, slab < slabs - 1)
+    to = (down, up)
+
+    barrier = pltpu.get_barrier_semaphore()
+    peers = [lax.rem(group + k, groups) for k in range(groups)]
+    for peer in peers[1:]:
+        pl.semaphore_signal(barrier, inc=1, device_id=(slab, peer), device_id_type=MESH)
+    for side in range(2):
+
+        @pl.when(has[side])
+        def _():
+            for peer in peers:
+                pl.semaphore_signal(barrier, inc=1, device_id=(to[side], peer), device_id_type=MESH)
+
+    for side in range(2):
+
+        @pl.when(jnp.logical_not(has[side]))
+        def _():
+            got_side[side] = jnp.zeros(got_side.shape[1:], jnp.float32)
+            for sweep in range(SWEEPS):
+                in_side[sweep, side] = jnp.zeros(in_side.shape[2:], jnp.float32)
+
+    sides = has[0].astype(jnp.int32) + has[1].astype(jnp.int32)
+    pl.semaphore_wait(barrier, groups - 1 + groups * sides)
+
+    side_copies = [
+        [
+            pltpu.make_async_remote_copy(
+                src_ref=send_ref.at[side],
+                dst_ref=got_side.at[1 - side, k],
+                send_sem=side_send.at[side, k],
+                recv_sem=side_recv.at[1 - side, k],
+                device_id=(to[side], peers[k]),
+                device_id_type=MESH,
+            )
+            for k in range(groups)
+        ]
+        for side in range(2)
+    ]
+    own_copies = [
+        pltpu.make_async_remote_copy(
+            src_ref=send_ref,
+            dst_ref=got_own.at[k - 1],
+            send_sem=own_send.at[k - 1],
+            recv_sem=own_recv.at[k - 1],
+            device_id=(slab, peers[k]),
+            device_id_type=MESH,
+        )
+        for k in range(1, groups)
+    ]
+    for side in range(2):
+
+        @pl.when(has[side])
+        def _():
+            for copy in side_copies[side]:
+                copy.start()
+
+    for copy in own_copies:
+        copy.start()
+
+    sub = rows_of((8, LANES))
+    own_hot = one_hot(pos_ref[...])
+
+    def planes(low, high):
+        return jnp.where(sub < 4, spread(low), spread(high))
+
+    for copy in own_copies:
+        copy.wait_recv()
+    for side in range(2):
+
+        @pl.when(has[side])
+        def _():
+            for copy in side_copies[1 - side]:
+                copy.wait_recv()
+
+    sums = []
+    for plane in range(2):
+        total = send_ref[plane]
+        for k in range(groups - 1):
+            total = total + got_own[k, plane]
+        extra = got_side[plane, 0]
+        for k in range(1, groups):
+            extra = extra + got_side[plane, k]
+        sums.append(total + extra)
+    rhs = planes(sums[0][0:1], sums[1][0:1])
+    diag = planes(sums[0][1:2], sums[1][1:2])
+    real = lax.broadcasted_iota(jnp.int32, (8, LANES), 1) < POINTS
+    inverse = 1.0 / jnp.where(real, diag, 1.0)
+
+    theta = 0.5 * (lam_high + lam_low)
+    delta = 0.5 * (lam_high - lam_low)
+    sigma = theta / delta
+    direction = inverse * rhs * (1.0 / theta)
+    answer = direction
+    remain = rhs
+    rho = 1.0 / sigma
+    faces = []
+    for sweep in range(SWEEPS):
+        corners = corner_values(direction)
+        product = lex_ref[0] * spread(corners[0:1])
+        for q in range(1, 8):
+            product = product + lex_ref[q] * spread(corners[q : q + 1])
+        nodes = gather_sums(product)
+        for side in range(2):
+            out_side[sweep, side] = nodes[4 * side : 4 * side + 1]
+        pair = [
+            pltpu.make_async_remote_copy(
+                src_ref=out_side.at[sweep, side],
+                dst_ref=in_side.at[sweep, 1 - side],
+                send_sem=face_send.at[sweep, side],
+                recv_sem=face_recv.at[sweep, 1 - side],
+                device_id=(to[side], group),
+                device_id_type=MESH,
+            )
+            for side in range(2)
+        ]
+        faces.append(pair)
+        for side in range(2):
+
+            @pl.when(has[side])
+            def _():
+                pair[side].start()
+
+        for side in range(2):
+
+            @pl.when(has[side])
+            def _():
+                pair[1 - side].wait_recv()
+
+        remain = remain - (nodes + planes(in_side[sweep, 0], in_side[sweep, 1]))
+        rho_new = 1.0 / (2.0 * sigma - rho)
+        direction = rho_new * rho * direction + 2.0 * rho_new / delta * inverse * remain
+        answer = answer + direction
+        rho = rho_new
+
+    picked = join_parts(jnp.dot(parts_of(corner_values(answer)), own_hot, preferred_element_type=jnp.float32))
+    fine = jnp.concatenate([table_ref[...], table_ref[...]], axis=0)
+    half = rows_of((8, 1)) < 4
+    for h in range(2):
+        weights = [
+            jnp.broadcast_to(jnp.where(half, i31_ref[2 * h, j], i31_ref[2 * h + 1, j]) * fine[:, k : k + 1], (8, 128))
+            for j in range(2)
+            for k in range(2)
+        ]
+        for a in range(4):
+            value = i31_ref[a, 0] * picked[0:4] + i31_ref[a, 1] * picked[4:8]
+            block = sum(weights[q] * spread(value[q : q + 1]) for q in range(4))
+            out_ref[8 * (2 * a + h) : 8 * (2 * a + h) + 8, :] = block
+
+    for copy in own_copies:
+        copy.wait_send()
+    for side in range(2):
+
+        @pl.when(has[side])
+        def _():
+            for copy in side_copies[side]:
+                copy.wait_send()
+            for pair in faces:
+                pair[side].wait_send()
+
+
+def one_layer(resid7, interp73, interp31, elem_ops, conn):
+    slabs, groups = (lax.axis_size("slab"), lax.axis_size("grp"))
+    lex, send, place = pl.pallas_call(
+        setup_kernel,
+        out_shape=(
+            jax.ShapeDtypeStruct((8, 8, LANES), jnp.float32),
+            jax.ShapeDtypeStruct((2, 2, LANES), jnp.float32),
+            jax.ShapeDtypeStruct((1, 128), jnp.int32),
+        ),
+        in_specs=[VMEM] * 4 + [SMEM] * 2,
+        out_specs=(VMEM,) * 3,
+    )(conn, elem_ops, resid7, interp73, interp73, interp31)
+    dma = pltpu.SemaphoreType.DMA
+    return pl.pallas_call(
+        functools.partial(smooth_kernel, slabs, groups),
+        out_shape=jax.ShapeDtypeStruct((64, 128), jnp.float32),
+        in_specs=[VMEM] * 4 + [SMEM],
+        out_specs=VMEM,
+        scratch_shapes=[
+            pltpu.VMEM((groups - 1, 2, 2, LANES), jnp.float32),
+            pltpu.VMEM((2, groups, 2, LANES), jnp.float32),
+            pltpu.VMEM((SWEEPS, 2, 1, LANES), jnp.float32),
+            pltpu.VMEM((SWEEPS, 2, 1, LANES), jnp.float32),
+            dma((groups - 1,)),
+            dma((groups - 1,)),
+            dma((2, groups)),
+            dma((2, groups)),
+            dma((SWEEPS, 2)),
+            dma((SWEEPS, 2)),
+        ],
+        compiler_params=pltpu.CompilerParams(collective_id=0, has_side_effects=True),
+    )(send, lex, place, interp31, interp31)
+
+
+def dispatch(resid7, interp73, interp31, elem_ops, conn, faces):
+    if conn.shape[1] == LINE and resid7.shape[1] == 128 and lax.axis_size("grp") > 1:
+        return one_layer(resid7, interp73, interp31, elem_ops, conn)
+    return local(resid7, interp73, interp31, elem_ops, conn, faces)
+
+
 def solution(mesh):
     in_specs = (
         P(None, ("slab", "grp")),
@@ -117,4 +454,4 @@
         P(None, "slab", None),
     )
     out_specs = P(None, ("slab", "grp"))
-    return jax.shard_map(local, mesh=mesh, in_specs=in_specs, out_specs=out_specs, check_vma=False)
+    return jax.shard_map(dispatch, mesh=mesh, in_specs=in_specs, out_specs=out_specs, check_vma=False)

time: 225 us -> 22.4 us (0.10)
  the two profiles are of different devices: /device:TPU:0 before, /device:TPU:4 now
where the time goes in v1:
time: 22.4 us; the launch traced here: 22.1 us
  Pallas kernels  18.8 us (84%)
  local copies, waits for them, and re-layouts  3.37 us (15%)
    pallas_call x1, Pallas kernels, one_layer(): pl.pallas_call(functools.partial(smooth_kernel, slabs, groups), out_shape...  15.8 us
    unnamed x5, local copies, waits for them, and re-layouts  3.37 us
    pallas_call x1, Pallas kernels, one_layer(): pl.pallas_call(setup_kernel, out_shape=(jax.ShapeDtypeStruct((8, 8, LANES...  2.94 us

profile of v1, /device:TPU:4, one launch (start us, length us, event | category | flops | bytes accessed | tf_op | source)
XLA Modules:
  0.0 22.1 jit_solution(6465043558416287024)
XLA Ops:
  0.0 0.0 copy-start
  0.0 1.3 %copy.8.i31_ref.table_ref = f32[4,2]{1,0:T(4,128)} copy(f32[4,2]{0,1:T(2,128)} %param.8) | data formatting | bytes 64 | tf_op args[2]
  1.3 0.0 copy-done
  1.3 0.7 %copy.6.table_ref.i73_ref = f32[8,4]{1,0:T(8,128)} copy(f32[8,4]{0,1:T(4,128)S(1)} %copy-done) | data formatting | bytes 256 | tf_op args[1]
  2.0 2.9 %shard_map.55 = (f32[8,8,640]{2,1,0:T(8,128)}, f32[2,2,640]{2,1,0:T(2,128)}, s32[1,128]{1,0:T(1,128)}) custom-call(s32[8,512]{1,0:T(8,128)} %conn_ref.1, f32[8,8,512]{2,1,0:T(8,128)} %ops_ref.1, f32[512,128]{1,0:T(8,128)} %res_ref.1, f32[8,4]{1,0:T(8,128)} %copy.6.table_ref.i73_ref, f32[8,4]{1,0:T(8,128)} %copy.6.table_ref.i73_ref, f32[4,2]{1,0:T(4,128)} %copy.8.i31_ref.table_ref), custom_call_target="tpu_custom_call" | custom-call | tf_op jit(solution)/shard_map/pallas_call | solution.py:409
  4.9 15.8 %shard_map.56 = f32[64,128]{1,0:T(8,128)} custom-call(f32[2,2,640]{2,1,0:T(2,128)} %get-tuple-element.8.send_ref, f32[8,8,640]{2,1,0:T(8,128)} %get-tuple-element.9.lex_ref, s32[1,128]{1,0:T(1,128)} %get-tuple-element.10.pos_ref, f32[4,2]{1,0:T(4,128)} %copy.8.i31_ref.table_ref, f32[4,2]{1,0:T(4,128)} %copy.8.i31_ref.table_ref), custom_call_target="tpu_custom_call" | custom-call | tf_op jit(solution)/shard_map/pallas_call | solution.py:420
  20.8 1.4 %copy.12 = f32[64,128]{1,0:T(8,128)} copy(f32[64,128]{1,0:T(8,128)} %shard_map.56) | data formatting | bytes 65536
Async XLA Ops:
  0.0 1.3 %copy-start = (f32[8,4]{0,1:T(4,128)S(1)}, f32[8,4]{0,1:T(4,128)}, u32[]{:S(2)}) copy-start(f32[8,4]{0,1:T(4,128)} %param.7) | copy-start | bytes 388

commit v2 on v1

--- a/solution.py
+++ b/solution.py
@@ -202,16 +202,43 @@
     return jnp.where(rows_of((LANES, row.shape[1])) == spread(row, LANES), 1.0, 0.0).astype(jnp.bfloat16)
 
 
-def setup_kernel(conn_ref, ops_ref, res_ref, table_ref, i73_ref, i31_ref, lex_ref, send_ref, pos_ref):
-    group = lax.axis_index("grp")
-    coef = [[sum(i73_ref[i, m] * i31_ref[m, a] for m in range(4)) for a in range(2)] for i in range(8)]
-    place = positions(conn_ref[...])
-
+def cycle_kernel(slabs, groups, conn_ref, ops_ref, res_ref, i73_ref, i31_ref, out_ref, lex_ref, send_ref, got_own, got_side, out_side, in_side, own_send, own_recv, side_send, side_recv, face_send, face_recv):
+    slab, group = (lax.axis_index("slab"), lax.axis_index("grp"))
+    down, up = (lax.rem(slab + slabs - 1, slabs), lax.rem(slab + 1, slabs))
+    has = (slab > 0, slab < slabs - 1)
+    to = (down, up)
+
+    barrier = pltpu.get_barrier_semaphore()
+    peers = [lax.rem(group + k, groups) for k in range(groups)]
+    for peer in peers[1:]:
+        pl.semaphore_signal(barrier, inc=1, device_id=(slab, peer), device_id_type=MESH)
+    for side in range(2):
+
+        @pl.when(has[side])
+        def _():
+            for peer in peers:
+                pl.semaphore_signal(barrier, inc=1, device_id=(to[side], peer), device_id_type=MESH)
+
+    for side in range(2):
+
+        @pl.when(jnp.logical_not(has[side]))
+        def _():
+            got_side[side] = jnp.zeros(got_side.shape[1:], jnp.float32)
+            for sweep in range(SWEEPS):
+                in_side[sweep, side] = jnp.zeros(in_side.shape[2:], jnp.float32)
+
+    coef = [[sum(i73_ref[m, i] * i31_ref[a, m] for m in range(4)) for a in range(2)] for i in range(8)]
     along_j = [[None] * 8, [None] * 8]
     for j in range(8):
         for a in range(2):
             along_j[a][j] = sum(coef[i][a] * res_ref[64 * i + 8 * j : 64 * i + 8 * j + 8, :] for i in range(8))
-    last = [sum(table_ref[:, m : m + 1] * i31_ref[m, c] for m in range(4)) for c in range(2)]
+    sub_tile = rows_of((8, 128))
+    last = []
+    for c in range(2):
+        column = jnp.full((8, 128), coef[0][c], jnp.float32)
+        for k in range(1, 8):
+            column = jnp.where(sub_tile == k, coef[k][c], column)
+        last.append(column)
     rows = []
     for a in range(2):
         for b in range(2):
@@ -222,10 +249,10 @@
     lanes = pl.ds(pl.multiple_of(group * 128, 128), 128)
     diagonal = stack_rows([ops_ref[p, p : p + 1, lanes] for p in range(8)])
 
+    place = positions(conn_ref[...])
     mine = spread(place[0:1])
     for b in range(1, BLOCKS):
         mine = jnp.where(group == b, spread(place[b : b + 1]), mine)
-    pos_ref[...] = mine[0:1]
     own_hot = one_hot(mine[0:1])
     both = parts_of(jnp.concatenate([low_res, diagonal], axis=0))
     both = join_parts(lax.dot_general(both, own_hot, (((1,), (1,)), ((), ())), preferred_element_type=jnp.float32))
@@ -233,37 +260,6 @@
         nodes = gather_sums(both[8 * at : 8 * at + 8])
         for plane in range(2):
             send_ref[plane, at : at + 1, :] = nodes[4 * plane : 4 * plane + 1]
-
-    hot = jnp.concatenate([one_hot(place[b : b + 1]) for b in range(BLOCKS)], axis=1)
-    ops = parts_of(ops_ref[...].reshape(64, LINE))
-    lex = lax.dot_general(ops, hot, (((1,), (1,)), ((), ())), preferred_element_type=jnp.float32)
-    lex_ref[...] = join_parts(lex).reshape(8, 8, LANES)
-
-
-def smooth_kernel(slabs, groups, send_ref, lex_ref, pos_ref, table_ref, i31_ref, out_ref, got_own, got_side, out_side, in_side, own_send, own_recv, side_send, side_recv, face_send, face_recv):
-    slab, group = (lax.axis_index("slab"), lax.axis_index("grp"))
-    down, up = (lax.rem(slab + slabs - 1, slabs), lax.rem(slab + 1, slabs))
-    has = (slab > 0, slab < slabs - 1)
-    to = (down, up)
-
-    barrier = pltpu.get_barrier_semaphore()
-    peers = [lax.rem(group + k, groups) for k in range(groups)]
-    for peer in peers[1:]:
-        pl.semaphore_signal(barrier, inc=1, device_id=(slab, peer), device_id_type=MESH)
-    for side in range(2):
-
-        @pl.when(has[side])
-        def _():
-            for peer in peers:
-                pl.semaphore_signal(barrier, inc=1, device_id=(to[side], peer), device_id_type=MESH)
-
-    for side in range(2):
-
-        @pl.when(jnp.logical_not(has[side]))
-        def _():
-            got_side[side] = jnp.zeros(got_side.shape[1:], jnp.float32)
-            for sweep in range(SWEEPS):
-                in_side[sweep, side] = jnp.zeros(in_side.shape[2:], jnp.float32)
 
     sides = has[0].astype(jnp.int32) + has[1].astype(jnp.int32)
     pl.semaphore_wait(barrier, groups - 1 + groups * sides)
@@ -304,7 +300,10 @@
         copy.start()
 
     sub = rows_of((8, LANES))
-    own_hot = one_hot(pos_ref[...])
+    hot = jnp.concatenate([one_hot(place[b : b + 1]) for b in range(BLOCKS)], axis=1)
+    ops = parts_of(ops_ref[...].reshape(64, LINE))
+    lex = lax.dot_general(ops, hot, (((1,), (1,)), ((), ())), preferred_element_type=jnp.float32)
+    lex_ref[...] = join_parts(lex).reshape(8, 8, LANES)
 
     def planes(low, high):
         return jnp.where(sub < 4, spread(low), spread(high))
@@ -378,19 +377,7 @@
         answer = answer + direction
         rho = rho_new
 
-    picked = join_parts(jnp.dot(parts_of(corner_values(answer)), own_hot, preferred_element_type=jnp.float32))
-    fine = jnp.concatenate([table_ref[...], table_ref[...]], axis=0)
-    half = rows_of((8, 1)) < 4
-    for h in range(2):
-        weights = [
-            jnp.broadcast_to(jnp.where(half, i31_ref[2 * h, j], i31_ref[2 * h + 1, j]) * fine[:, k : k + 1], (8, 128))
-            for j in range(2)
-            for k in range(2)
-        ]
-        for a in range(4):
-            value = i31_ref[a, 0] * picked[0:4] + i31_ref[a, 1] * picked[4:8]
-            block = sum(weights[q] * spread(value[q : q + 1]) for q in range(4))
-            out_ref[8 * (2 * a + h) : 8 * (2 * a + h) + 8, :] = block
+    out_ref[...] = join_parts(jnp.dot(parts_of(corner_values(answer)), own_hot, preferred_element_type=jnp.float32))
 
     for copy in own_copies:
         copy.wait_send()
@@ -404,25 +391,34 @@
                 pair[side].wait_send()
 
 
+def prolong_kernel(picked_ref, i31_ref, out_ref):
+    picked = picked_ref[...]
+    sub = rows_of((8, 128))
+    fine = []
+    for k in range(2):
+        column = jnp.full((8, 128), i31_ref[k, 0], jnp.float32)
+        for c in range(1, 4):
+            column = jnp.where(sub % 4 == c, i31_ref[k, c], column)
+        fine.append(column)
+    for h in range(2):
+        weights = [jnp.where(sub < 4, i31_ref[j, 2 * h], i31_ref[j, 2 * h + 1]) * fine[k] for j in range(2) for k in range(2)]
+        for a in range(4):
+            value = i31_ref[0, a] * picked[0:4] + i31_ref[1, a] * picked[4:8]
+            block = sum(weights[q] * spread(value[q : q + 1]) for q in range(4))
+            out_ref[8 * (2 * a + h) : 8 * (2 * a + h) + 8, :] = block
+
+
 def one_layer(resid7, interp73, interp31, elem_ops, conn):
     slabs, groups = (lax.axis_size("slab"), lax.axis_size("grp"))
-    lex, send, place = pl.pallas_call(
-        setup_kernel,
-        out_shape=(
-            jax.ShapeDtypeStruct((8, 8, LANES), jnp.float32),
-            jax.ShapeDtypeStruct((2, 2, LANES), jnp.float32),
-            jax.ShapeDtypeStruct((1, 128), jnp.int32),
-        ),
-        in_specs=[VMEM] * 4 + [SMEM] * 2,
-        out_specs=(VMEM,) * 3,
-    )(conn, elem_ops, resid7, interp73, interp73, interp31)
     dma = pltpu.SemaphoreType.DMA
-    return pl.pallas_call(
-        functools.partial(smooth_kernel, slabs, groups),
-        out_shape=jax.ShapeDtypeStruct((64, 128), jnp.float32),
-        in_specs=[VMEM] * 4 + [SMEM],
+    picked = pl.pallas_call(
+        functools.partial(cycle_kernel, slabs, groups),
+        out_shape=jax.ShapeDtypeStruct((8, 128), jnp.float32),
+        in_specs=[VMEM] * 3 + [SMEM] * 2,
         out_specs=VMEM,
         scratch_shapes=[
+            pltpu.VMEM((8, 8, LANES), jnp.float32),
+            pltpu.VMEM((2, 2, LANES), jnp.float32),
             pltpu.VMEM((groups - 1, 2, 2, LANES), jnp.float32),
             pltpu.VMEM((2, groups, 2, LANES), jnp.float32),
             pltpu.VMEM((SWEEPS, 2, 1, LANES), jnp.float32),
@@ -435,7 +431,13 @@
             dma((SWEEPS, 2)),
         ],
         compiler_params=pltpu.CompilerParams(collective_id=0, has_side_effects=True),
-    )(send, lex, place, interp31, interp31)
+    )(conn, elem_ops, resid7, interp73.T, interp31.T)
+    return pl.pallas_call(
+        prolong_kernel,
+        out_shape=jax.ShapeDtypeStruct((64, 128), jnp.float32),
+        in_specs=[VMEM, SMEM],
+        out_specs=VMEM,
+    )(picked, interp31.T)
 
 
 def dispatch(resid7, interp73, interp31, elem_ops, conn, faces):

time: 22.4 us -> 17.6 us (0.79)
  local copies, waits for them, and re-layouts: 3.37 us -> 0 us
  Pallas kernels: 18.8 us -> 17.4 us
    unnamed x5 -> x0, local copies, waits for them, and re-layouts: 3.37 us -> none
    pallas_call x2, Pallas kernels: 18.8 us -> 17.4 us  [the longest x1 16 us: one_layer(): pl.pallas_call(functools.partial(cycle_kernel, slabs, groups), out_shape=...]
where the time goes in v2:
time: 17.6 us; the launch traced here: 17.4 us
  Pallas kernels  17.4 us (99%)
    pallas_call x1, Pallas kernels, one_layer(): pl.pallas_call(functools.partial(cycle_kernel, slabs, groups), out_shape=...  16 us
    pallas_call x1, Pallas kernels, one_layer(): pl.pallas_call(prolong_kernel, out_shape=jax.ShapeDtypeStruct((64, 128),...  1.46 us

profile of v2, /device:TPU:4, one launch (start us, length us, event | category | flops | bytes accessed | tf_op | source)
XLA Modules:
  0.0 17.4 jit_solution(7522637456550342695)
XLA Ops:
  0.0 16.0 %shard_map.55.picked_ref = f32[8,128]{1,0:T(8,128)} custom-call(s32[8,512]{1,0:T(8,128)} %conn_ref.1, f32[8,8,512]{2,1,0:T(8,128)} %ops_ref.1, f32[512,128]{1,0:T(8,128)} %res_ref.1, f32[4,8]{1,0:T(4,128)} %bitcast.4, f32[2,4]{1,0:T(2,128)} %bitcast.2), custom_call_target="tpu_custom_call" | custom-call | tf_op jit(solution)/shard_map/pallas_call | solution.py:414
  16.0 1.5 %shard_map.56 = f32[64,128]{1,0:T(8,128)} custom-call(f32[8,128]{1,0:T(8,128)} %shard_map.55.picked_ref, f32[2,4]{1,0:T(2,128)} %bitcast.3), custom_call_target="tpu_custom_call" | custom-call | tf_op jit(solution)/shard_map/pallas_call | solution.py:435

commit v3 on v2

--- a/solution.py
+++ b/solution.py
@@ -202,11 +202,13 @@
     return jnp.where(rows_of((LANES, row.shape[1])) == spread(row, LANES), 1.0, 0.0).astype(jnp.bfloat16)
 
 
-def cycle_kernel(slabs, groups, conn_ref, ops_ref, res_ref, i73_ref, i31_ref, out_ref, lex_ref, send_ref, got_own, got_side, out_side, in_side, own_send, own_recv, side_send, side_recv, face_send, face_recv):
+def cycle_kernel(slabs, groups, conn_ref, ops_ref, res_ref, i73_ref, i31_ref, out_ref, lex_ref, near_ref, send_ref, got_own, got_side, out_pack, in_pack, out_far, in_far, own_send, own_recv, side_send, side_recv, ops_send, ops_recv, pack_send, pack_recv, far_send, far_recv):
     slab, group = (lax.axis_index("slab"), lax.axis_index("grp"))
     down, up = (lax.rem(slab + slabs - 1, slabs), lax.rem(slab + 1, slabs))
     has = (slab > 0, slab < slabs - 1)
     to = (down, up)
+    beyond = (slab > 1, slab < slabs - 2)
+    skip = (lax.rem(slab + slabs - 2, slabs), lax.rem(slab + 2, slabs))
 
     barrier = pltpu.get_barrier_semaphore()
     peers = [lax.rem(group + k, groups) for k in range(groups)]
@@ -219,13 +221,21 @@
             for peer in peers:
                 pl.semaphore_signal(barrier, inc=1, device_id=(to[side], peer), device_id_type=MESH)
 
+        @pl.when(beyond[side])
+        def _():
+            pl.semaphore_signal(barrier, inc=1, device_id=(skip[side], group), device_id_type=MESH)
+
     for side in range(2):
 
         @pl.when(jnp.logical_not(has[side]))
         def _():
             got_side[side] = jnp.zeros(got_side.shape[1:], jnp.float32)
-            for sweep in range(SWEEPS):
-                in_side[sweep, side] = jnp.zeros(in_side.shape[2:], jnp.float32)
+            in_pack[side] = jnp.where(rows_of((4, LANES)) == 3, 1.0, 0.0)
+            near_ref[:, 4 * side : 4 * side + 4, :] = jnp.zeros((8, 4, LANES), jnp.float32)
+
+        @pl.when(jnp.logical_not(beyond[side]))
+        def _():
+            in_far[side] = jnp.zeros((1, LANES), jnp.float32)
 
     coef = [[sum(i73_ref[m, i] * i31_ref[a, m] for m in range(4)) for a in range(2)] for i in range(8)]
     along_j = [[None] * 8, [None] * 8]
@@ -262,7 +272,8 @@
             send_ref[plane, at : at + 1, :] = nodes[4 * plane : 4 * plane + 1]
 
     sides = has[0].astype(jnp.int32) + has[1].astype(jnp.int32)
-    pl.semaphore_wait(barrier, groups - 1 + groups * sides)
+    far_sides = beyond[0].astype(jnp.int32) + beyond[1].astype(jnp.int32)
+    pl.semaphore_wait(barrier, groups - 1 + groups * sides + far_sides)
 
     side_copies = [
         [
@@ -304,6 +315,23 @@
     ops = parts_of(ops_ref[...].reshape(64, LINE))
     lex = lax.dot_general(ops, hot, (((1,), (1,)), ((), ())), preferred_element_type=jnp.float32)
     lex_ref[...] = join_parts(lex).reshape(8, 8, LANES)
+    ops_copies = []
+    for side in range(2):
+        ops_copies.append(
+            pltpu.make_async_remote_copy(
+                src_ref=lex_ref.at[:, pl.ds(4 * side, 4), :],
+                dst_ref=near_ref.at[:, pl.ds(4 - 4 * side, 4), :],
+                send_sem=ops_send.at[side],
+                recv_sem=ops_recv.at[1 - side],
+                device_id=(to[side], group),
+                device_id_type=MESH,
+            )
+        )
+
+        @pl.when(has[side])
+        def _():
+            ops_copies[side].start()
+
 
     def planes(low, high):
         return jnp.where(sub < 4, spread(low), spread(high))
@@ -334,48 +362,83 @@
     theta = 0.5 * (lam_high + lam_low)
     delta = 0.5 * (lam_high - lam_low)
     sigma = theta / delta
-    direction = inverse * rhs * (1.0 / theta)
-    answer = direction
-    remain = rhs
-    rho = 1.0 / sigma
-    faces = []
-    for sweep in range(SWEEPS):
-        corners = corner_values(direction)
-        product = lex_ref[0] * spread(corners[0:1])
-        for q in range(1, 8):
-            product = product + lex_ref[q] * spread(corners[q : q + 1])
-        nodes = gather_sums(product)
-        for side in range(2):
-            out_side[sweep, side] = nodes[4 * side : 4 * side + 1]
-        pair = [
+    first = inverse * rhs * (1.0 / theta)
+    corners = corner_values(first)
+    product = lex_ref[0] * spread(corners[0:1])
+    for q in range(1, 8):
+        product = product + lex_ref[q] * spread(corners[q : q + 1])
+    nodes = gather_sums(product)
+    pack_copies, far_copies = ([], [])
+    for side in range(2):
+        near, far = (4 * side, 4 - 4 * side)
+        for at, value in enumerate((nodes[near : near + 1], nodes[far : far + 1], rhs[far : far + 1], diag[far : far + 1])):
+            out_pack[side, at : at + 1, :] = value
+        out_far[side] = nodes[near : near + 1]
+        pack_copies.append(
             pltpu.make_async_remote_copy(
-                src_ref=out_side.at[sweep, side],
-                dst_ref=in_side.at[sweep, 1 - side],
-                send_sem=face_send.at[sweep, side],
-                recv_sem=face_recv.at[sweep, 1 - side],
+                src_ref=out_pack.at[side],
+                dst_ref=in_pack.at[1 - side],
+                send_sem=pack_send.at[side],
+                recv_sem=pack_recv.at[1 - side],
                 device_id=(to[side], group),
                 device_id_type=MESH,
             )
-            for side in range(2)
-        ]
-        faces.append(pair)
-        for side in range(2):
-
-            @pl.when(has[side])
-            def _():
-                pair[side].start()
-
-        for side in range(2):
-
-            @pl.when(has[side])
-            def _():
-                pair[1 - side].wait_recv()
-
-        remain = remain - (nodes + planes(in_side[sweep, 0], in_side[sweep, 1]))
-        rho_new = 1.0 / (2.0 * sigma - rho)
-        direction = rho_new * rho * direction + 2.0 * rho_new / delta * inverse * remain
-        answer = answer + direction
-        rho = rho_new
+        )
+        far_copies.append(
+            pltpu.make_async_remote_copy(
+                src_ref=out_far.at[side],
+                dst_ref=in_far.at[1 - side],
+                send_sem=far_send.at[side],
+                recv_sem=far_recv.at[1 - side],
+                device_id=(skip[side], group),
+                device_id_type=MESH,
+            )
+        )
+
+        @pl.when(beyond[side])
+        def _():
+            far_copies[side].start()
+
+        @pl.when(has[side])
+        def _():
+            pack_copies[side].start()
+
+    for side in range(2):
+
+        @pl.when(has[side])
+        def _():
+            ops_copies[1 - side].wait_recv()
+            pack_copies[1 - side].wait_recv()
+
+        @pl.when(beyond[side])
+        def _():
+            far_copies[1 - side].wait_recv()
+
+    low, high = (in_pack[0], in_pack[1])
+    far_inverse = 1.0 / jnp.where(real, planes(low[3:4], high[3:4]), 1.0)
+    far_rhs = planes(low[2:3], high[2:3])
+    far_first = far_inverse * far_rhs * (1.0 / theta)
+    far_remain = far_rhs - planes(low[1:2] + in_far[0], high[1:2] + in_far[1])
+    remain = rhs - (nodes + planes(low[0:1], high[0:1]))
+    rho = 1.0 / sigma
+    rho_new = 1.0 / (2.0 * sigma - rho)
+    second = rho_new * rho * first + 2.0 * rho_new / delta * inverse * remain
+    far_second = rho_new * rho * far_first + 2.0 * rho_new / delta * far_inverse * far_remain
+    rho = rho_new
+    rho_new = 1.0 / (2.0 * sigma - rho)
+
+    corners = corner_values(second)
+    ends = (jnp.where(sub < 4, far_second, second), jnp.where(sub < 4, second, far_second))
+    product = lex_ref[0] * spread(corners[0:1])
+    for q in range(1, 8):
+        product = product + lex_ref[q] * spread(corners[q : q + 1])
+    for q in range(8):
+        shift = q // 2 % 2 * STRIDE + q % 2
+        value = ends[q // 4]
+        product = product + near_ref[q] * (pltpu.roll(value, LANES - shift, 1) if shift else value)
+    remain = remain - gather_sums(product)
+    third = rho_new * rho * second + 2.0 * rho_new / delta * inverse * remain
+    answer = first + second + third
 
     out_ref[...] = join_parts(jnp.dot(parts_of(corner_values(answer)), own_hot, preferred_element_type=jnp.float32))
 
@@ -387,8 +450,12 @@
         def _():
             for copy in side_copies[side]:
                 copy.wait_send()
-            for pair in faces:
-                pair[side].wait_send()
+            ops_copies[side].wait_send()
+            pack_copies[side].wait_send()
+
+        @pl.when(beyond[side])
+        def _():
+            far_copies[side].wait_send()
 
 
 def prolong_kernel(picked_ref, i31_ref, out_ref):
@@ -413,22 +480,29 @@
     dma = pltpu.SemaphoreType.DMA
     picked = pl.pallas_call(
         functools.partial(cycle_kernel, slabs, groups),
-        out_shape=jax.ShapeDtypeStruct((8, 128), jnp.float32),
+        out_shape=pltpu.VMEM((8, 128), jnp.float32),
         in_specs=[VMEM] * 3 + [SMEM] * 2,
         out_specs=VMEM,
         scratch_shapes=[
             pltpu.VMEM((8, 8, LANES), jnp.float32),
+            pltpu.VMEM((8, 8, LANES), jnp.float32),
             pltpu.VMEM((2, 2, LANES), jnp.float32),
             pltpu.VMEM((groups - 1, 2, 2, LANES), jnp.float32),
             pltpu.VMEM((2, groups, 2, LANES), jnp.float32),
-            pltpu.VMEM((SWEEPS, 2, 1, LANES), jnp.float32),
-            pltpu.VMEM((SWEEPS, 2, 1, LANES), jnp.float32),
+            pltpu.VMEM((2, 4, LANES), jnp.float32),
+            pltpu.VMEM((2, 4, LANES), jnp.float32),
+            pltpu.VMEM((2, 1, LANES), jnp.float32),
+            pltpu.VMEM((2, 1, LANES), jnp.float32),
             dma((groups - 1,)),
             dma((groups - 1,)),
             dma((2, groups)),
             dma((2, groups)),
-            dma((SWEEPS, 2)),
-            dma((SWEEPS, 2)),
+            dma((2,)),
+            dma((2,)),
+            dma((2,)),
+            dma((2,)),
+            dma((2,)),
+            dma((2,)),
         ],
         compiler_params=pltpu.CompilerParams(collective_id=0, has_side_effects=True),
     )(conn, elem_ops, resid7, interp73.T, interp31.T)
@@ -437,7 +511,7 @@
         out_shape=jax.ShapeDtypeStruct((64, 128), jnp.float32),
         in_specs=[VMEM, SMEM],
         out_specs=VMEM,
-    )(picked, interp31.T)
+    )(pltpu.with_memory_space_constraint(picked, pltpu.VMEM), interp31.T)
 
 
 def dispatch(resid7, interp73, interp31, elem_ops, conn, faces):

time: 17.6 us -> 15.6 us (0.89)
  the two profiles are of different devices: /device:TPU:4 before, /device:TPU:0 now
where the time goes in v3:
time: 15.6 us; the launch traced here: 15.4 us
  Pallas kernels  15.4 us (99%)
    pallas_call x1, Pallas kernels, one_layer(): pl.pallas_call(functools.partial(cycle_kernel, slabs, groups), out_shape=...  14.1 us
    pallas_call x1, Pallas kernels, one_layer(): pl.pallas_call(prolong_kernel, out_shape=jax.ShapeDtypeStruct((64, 128),...  1.32 us

profile of v3, /device:TPU:0, one launch (start us, length us, event | category | flops | bytes accessed | tf_op | source)
XLA Modules:
  0.0 15.4 jit_solution(5773966034197177907)
XLA Ops:
  0.0 14.1 %shard_map.55.picked_ref = f32[8,128]{1,0:T(8,128)S(1)} custom-call(s32[8,512]{1,0:T(8,128)} %conn_ref.1, f32[8,8,512]{2,1,0:T(8,128)} %ops_ref.1, f32[512,128]{1,0:T(8,128)} %res_ref.1, f32[4,8]{1,0:T(4,128)} %bitcast.4, f32[2,4]{1,0:T(2,128)} %bitcast.2), custom_call_target="tpu_custom_call" | custom-call | tf_op jit(solution)/shard_map/pallas_call | solution.py:481
  14.1 1.3 %shard_map.56 = f32[64,128]{1,0:T(8,128)} custom-call(f32[8,128]{1,0:T(8,128)S(1)} %shard_map.55.picked_ref, f32[2,4]{1,0:T(2,128)} %bitcast.3), custom_call_target="tpu_custom_call" | custom-call | tf_op jit(solution)/shard_map/pallas_call | solution.py:509

commit v4 on v3

--- a/solution.py
+++ b/solution.py
@@ -202,7 +202,7 @@
     return jnp.where(rows_of((LANES, row.shape[1])) == spread(row, LANES), 1.0, 0.0).astype(jnp.bfloat16)
 
 
-def cycle_kernel(slabs, groups, conn_ref, ops_ref, res_ref, i73_ref, i31_ref, out_ref, lex_ref, near_ref, send_ref, got_own, got_side, out_pack, in_pack, out_far, in_far, own_send, own_recv, side_send, side_recv, ops_send, ops_recv, pack_send, pack_recv, far_send, far_recv):
+def cycle_kernel(slabs, groups, conn_hbm, ops_hbm, res_hbm, i73_ref, i31_ref, out_ref, conn_ref, ops_ref, res_ref, load_sem, lex_ref, near_ref, send_ref, got_own, got_side, out_pack, in_pack, out_far, in_far, own_send, own_recv, side_send, side_recv, ops_send, ops_recv, pack_send, pack_recv, far_send, far_recv):
     slab, group = (lax.axis_index("slab"), lax.axis_index("grp"))
     down, up = (lax.rem(slab + slabs - 1, slabs), lax.rem(slab + 1, slabs))
     has = (slab > 0, slab < slabs - 1)
@@ -210,6 +210,13 @@
     beyond = (slab > 1, slab < slabs - 2)
     skip = (lax.rem(slab + slabs - 2, slabs), lax.rem(slab + 2, slabs))
 
+    loads = [
+        pltpu.make_async_copy(source, target, load_sem.at[at])
+        for at, (source, target) in enumerate(((conn_hbm, conn_ref), (res_hbm, res_ref), (ops_hbm, ops_ref)))
+    ]
+    for load in loads:
+        load.start()
+
     barrier = pltpu.get_barrier_semaphore()
     peers = [lax.rem(group + k, groups) for k in range(groups)]
     for peer in peers[1:]:
@@ -237,6 +244,10 @@
         def _():
             in_far[side] = jnp.zeros((1, LANES), jnp.float32)
 
+    loads[0].wait()
+    place = positions(conn_ref[...])
+    loads[1].wait()
+    loads[2].wait()
     coef = [[sum(i73_ref[m, i] * i31_ref[a, m] for m in range(4)) for a in range(2)] for i in range(8)]
     along_j = [[None] * 8, [None] * 8]
     for j in range(8):
@@ -259,7 +270,6 @@
     lanes = pl.ds(pl.multiple_of(group * 128, 128), 128)
     diagonal = stack_rows([ops_ref[p, p : p + 1, lanes] for p in range(8)])
 
-    place = positions(conn_ref[...])
     mine = spread(place[0:1])
     for b in range(1, BLOCKS):
         mine = jnp.where(group == b, spread(place[b : b + 1]), mine)
@@ -336,6 +346,13 @@
     def planes(low, high):
         return jnp.where(sub < 4, spread(low), spread(high))
 
+    fine = []
+    for k in range(2):
+        column = jnp.full((8, 128), i31_ref[k, 0], jnp.float32)
+        for c in range(1, 4):
+            column = jnp.where(sub_tile % 4 == c, i31_ref[k, c], column)
+        fine.append(column)
+    weights = [jnp.where(sub_tile < 4, i31_ref[j, 2 * h], i31_ref[j, 2 * h + 1]) * fine[k] for h in range(2) for j in range(2) for k in range(2)]
     for copy in own_copies:
         copy.wait_recv()
     for side in range(2):
@@ -440,7 +457,12 @@
     third = rho_new * rho * second + 2.0 * rho_new / delta * inverse * remain
     answer = first + second + third
 
-    out_ref[...] = join_parts(jnp.dot(parts_of(corner_values(answer)), own_hot, preferred_element_type=jnp.float32))
+    picked = join_parts(jnp.dot(parts_of(corner_values(answer)), own_hot, preferred_element_type=jnp.float32))
+    for h in range(2):
+        for a in range(4):
+            value = i31_ref[0, a] * picked[0:4] + i31_ref[1, a] * picked[4:8]
+            block = sum(weights[4 * h + q] * spread(value[q : q + 1]) for q in range(4))
+            out_ref[8 * (2 * a + h) : 8 * (2 * a + h) + 8, :] = block
 
     for copy in own_copies:
         copy.wait_send()
@@ -458,32 +480,19 @@
             far_copies[side].wait_send()
 
 
-def prolong_kernel(picked_ref, i31_ref, out_ref):
-    picked = picked_ref[...]
-    sub = rows_of((8, 128))
-    fine = []
-    for k in range(2):
-        column = jnp.full((8, 128), i31_ref[k, 0], jnp.float32)
-        for c in range(1, 4):
-            column = jnp.where(sub % 4 == c, i31_ref[k, c], column)
-        fine.append(column)
-    for h in range(2):
-        weights = [jnp.where(sub < 4, i31_ref[j, 2 * h], i31_ref[j, 2 * h + 1]) * fine[k] for j in range(2) for k in range(2)]
-        for a in range(4):
-            value = i31_ref[0, a] * picked[0:4] + i31_ref[1, a] * picked[4:8]
-            block = sum(weights[q] * spread(value[q : q + 1]) for q in range(4))
-            out_ref[8 * (2 * a + h) : 8 * (2 * a + h) + 8, :] = block
-
-
 def one_layer(resid7, interp73, interp31, elem_ops, conn):
     slabs, groups = (lax.axis_size("slab"), lax.axis_size("grp"))
     dma = pltpu.SemaphoreType.DMA
-    picked = pl.pallas_call(
+    return pl.pallas_call(
         functools.partial(cycle_kernel, slabs, groups),
-        out_shape=pltpu.VMEM((8, 128), jnp.float32),
-        in_specs=[VMEM] * 3 + [SMEM] * 2,
+        out_shape=pltpu.VMEM((64, 128), jnp.float32),
+        in_specs=[pl.BlockSpec(memory_space=pl.ANY)] * 3 + [SMEM] * 2,
         out_specs=VMEM,
         scratch_shapes=[
+            pltpu.VMEM((8, LINE), jnp.int32),
+            pltpu.VMEM((8, 8, LINE), jnp.float32),
+            pltpu.VMEM((512, 128), jnp.float32),
+            dma((3,)),
             pltpu.VMEM((8, 8, LANES), jnp.float32),
             pltpu.VMEM((8, 8, LANES), jnp.float32),
             pltpu.VMEM((2, 2, LANES), jnp.float32),
@@ -506,12 +515,6 @@
         ],
         compiler_params=pltpu.CompilerParams(collective_id=0, has_side_effects=True),
     )(conn, elem_ops, resid7, interp73.T, interp31.T)
-    return pl.pallas_call(
-        prolong_kernel,
-        out_shape=jax.ShapeDtypeStruct((64, 128), jnp.float32),
-        in_specs=[VMEM, SMEM],
-        out_specs=VMEM,
-    )(pltpu.with_memory_space_constraint(picked, pltpu.VMEM), interp31.T)
 
 
 def dispatch(resid7, interp73, interp31, elem_ops, conn, faces):

time: 15.6 us -> 14.9 us (0.955)
  Pallas kernels: 15.4 us -> 14 us
  local copies, waits for them, and re-layouts: 0 us -> 0.62 us
    pallas_call x1 -> x0, Pallas kernels: 1.32 us -> none  [one_layer(): pl.pallas_call(prolong_kernel, out_shape=jax.ShapeDtypeStruct((64, 128),...]
    unnamed x0 -> x1, local copies, waits for them, and re-layouts: none -> 0.62 us
where the time goes in v4:
time: 14.9 us; the launch traced here: 14.7 us
  Pallas kernels  14 us (94%)
  local copies, waits for them, and re-layouts  0.62 us (4%)
    pallas_call x1, Pallas kernels, one_layer(): pl.pallas_call(functools.partial(cycle_kernel, slabs, groups), out_shape=...  14 us
    unnamed x1, local copies, waits for them, and re-layouts  0.62 us

profile of v4, /device:TPU:0, one launch (start us, length us, event | category | flops | bytes accessed | tf_op | source)
XLA Modules:
  0.0 14.7 jit_solution(17002304825218793979)
XLA Ops:
  0.0 14.0 %shard_map.55 = f32[64,128]{1,0:T(8,128)S(1)} custom-call(s32[8,512]{1,0:T(8,128)} %conn_hbm.1, f32[8,8,512]{2,1,0:T(8,128)} %ops_hbm.1, f32[512,128]{1,0:T(8,128)} %res_hbm.1, f32[4,8]{1,0:T(4,128)} %bitcast.2, f32[2,4]{1,0:T(2,128)} %bitcast.3), custom_call_target="tpu_custom_call" | custom-call | tf_op jit(solution)/shard_map/pallas_call | solution.py:486
  14.1 0.6 %copy.7 = f32[64,128]{1,0:T(8,128)} copy(f32[64,128]{1,0:T(8,128)S(1)} %shard_map.55) | data formatting | bytes 65536

commit v5 on v4

--- a/solution.py
+++ b/solution.py
@@ -151,7 +151,7 @@
 
 def gather_sums(corners):
     sub = rows_of(corners.shape)
-    odd, second = (sub % 2 == 1, sub // 2 % 2 == 1)
+    odd, second = ((sub & 1) == 1, (sub & 2) == 2)
     part = jnp.where(odd, pltpu.roll(corners, 1, 1), corners)
     part = part + jnp.where(odd, pltpu.roll(part, 1, 0), pltpu.roll(part, 7, 0))
     part = jnp.where(second, pltpu.roll(part, STRIDE, 1), part)
@@ -160,8 +160,8 @@
 
 def corner_values(nodes):
     sub = rows_of(nodes.shape)
-    part = jnp.where(sub // 2 % 2 == 1, pltpu.roll(nodes, LANES - STRIDE, 1), nodes)
-    return jnp.where(sub % 2 == 1, pltpu.roll(part, LANES - 1, 1), part)
+    part = jnp.where((sub & 2) == 2, pltpu.roll(nodes, LANES - STRIDE, 1), nodes)
+    return jnp.where((sub & 1) == 1, pltpu.roll(part, LANES - 1, 1), part)
 
 
 def before(ids, mine, theirs):
@@ -187,14 +187,14 @@
     state = stack_rows(rows)
     sub = rows_of((8, 128))
     for _ in range((EX - 1).bit_length()):
-        target = state % LINE
-        lane, block = (target % 128, target // 128)
+        target = state & (LINE - 1)
+        lane, block = (target & 127, target >> 7)
         got = jnp.zeros((8, 128), jnp.int32)
         for b in range(BLOCKS):
             table = jnp.where(sub < BLOCKS, spread(state[b : b + 1]), spread(state[BLOCKS + b : BLOCKS + b + 1]))
             got = jnp.where(block == b, jnp.take_along_axis(table, lane, axis=1), got)
         state = got + (state - target)
-    steps = state // LINE
+    steps = state >> (LINE.bit_length() - 1)
     return steps + STRIDE * pltpu.roll(steps, 4, 0)
 
 
@@ -350,7 +350,7 @@
     for k in range(2):
         column = jnp.full((8, 128), i31_ref[k, 0], jnp.float32)
         for c in range(1, 4):
-            column = jnp.where(sub_tile % 4 == c, i31_ref[k, c], column)
+            column = jnp.where((sub_tile & 3) == c, i31_ref[k, c], column)
         fine.append(column)
     weights = [jnp.where(sub_tile < 4, i31_ref[j, 2 * h], i31_ref[j, 2 * h + 1]) * fine[k] for h in range(2) for j in range(2) for k in range(2)]
     for copy in own_copies:

time: 14.9 us -> 14.8 us (level)
  no operation moved by 1% of the time
where the time goes in v5:
time: 14.8 us; the launch traced here: 14.6 us
  Pallas kernels  14 us (95%)
  local copies, waits for them, and re-layouts  0.62 us (4%)
    pallas_call x1, Pallas kernels, one_layer(): pl.pallas_call(functools.partial(cycle_kernel, slabs, groups), out_shape=...  14 us
    unnamed x1, local copies, waits for them, and re-layouts  0.62 us

profile of v5, /device:TPU:0, one launch (start us, length us, event | category | flops | bytes accessed | tf_op | source)
XLA Modules:
  0.0 14.6 jit_solution(16393910603970999046)
XLA Ops:
  0.0 14.0 %shard_map.55 = f32[64,128]{1,0:T(8,128)S(1)} custom-call(s32[8,512]{1,0:T(8,128)} %conn_hbm.1, f32[8,8,512]{2,1,0:T(8,128)} %ops_hbm.1, f32[512,128]{1,0:T(8,128)} %res_hbm.1, f32[4,8]{1,0:T(4,128)} %bitcast.2, f32[2,4]{1,0:T(2,128)} %bitcast.3), custom_call_target="tpu_custom_call" | custom-call | tf_op jit(solution)/shard_map/pallas_call | solution.py:486
  14.0 0.6 %copy.7 = f32[64,128]{1,0:T(8,128)} copy(f32[64,128]{1,0:T(8,128)S(1)} %shard_map.55) | data formatting | bytes 65536

commit v6 on v5

--- a/solution.py
+++ b/solution.py
@@ -202,7 +202,7 @@
     return jnp.where(rows_of((LANES, row.shape[1])) == spread(row, LANES), 1.0, 0.0).astype(jnp.bfloat16)
 
 
-def cycle_kernel(slabs, groups, conn_hbm, ops_hbm, res_hbm, i73_ref, i31_ref, out_ref, conn_ref, ops_ref, res_ref, load_sem, lex_ref, near_ref, send_ref, got_own, got_side, out_pack, in_pack, out_far, in_far, own_send, own_recv, side_send, side_recv, ops_send, ops_recv, pack_send, pack_recv, far_send, far_recv):
+def cycle_kernel(slabs, groups, conn_hbm, ops_hbm, res_hbm, i73_ref, i31_ref, out_ref, conn_ref, ops_ref, res_ref, load_sem, lex_ref, near_ref, send_ref, got_own, got_side, out_pack, in_pack, out_far, in_far, own_send, own_recv, side_send, side_recv, ops_send, ops_recv, pack_send, pack_recv, far_send, far_recv, out_early, in_early, early_send, early_recv):
     slab, group = (lax.axis_index("slab"), lax.axis_index("grp"))
     down, up = (lax.rem(slab + slabs - 1, slabs), lax.rem(slab + 1, slabs))
     has = (slab > 0, slab < slabs - 1)
@@ -237,7 +237,8 @@
         @pl.when(jnp.logical_not(has[side]))
         def _():
             got_side[side] = jnp.zeros(got_side.shape[1:], jnp.float32)
-            in_pack[side] = jnp.where(rows_of((4, LANES)) == 3, 1.0, 0.0)
+            in_pack[side] = jnp.zeros((2, LANES), jnp.float32)
+            in_early[side] = jnp.where(rows_of((2, LANES)) == 1, 1.0, 0.0)
             near_ref[:, 4 * side : 4 * side + 4, :] = jnp.zeros((8, 4, LANES), jnp.float32)
 
         @pl.when(jnp.logical_not(beyond[side]))
@@ -380,6 +381,26 @@
     delta = 0.5 * (lam_high - lam_low)
     sigma = theta / delta
     first = inverse * rhs * (1.0 / theta)
+    early_copies = []
+    for side in range(2):
+        far = 4 - 4 * side
+        for at, value in enumerate((rhs[far : far + 1], diag[far : far + 1])):
+            out_early[side, at : at + 1, :] = value
+        early_copies.append(
+            pltpu.make_async_remote_copy(
+                src_ref=out_early.at[side],
+                dst_ref=in_early.at[1 - side],
+                send_sem=early_send.at[side],
+                recv_sem=early_recv.at[1 - side],
+                device_id=(to[side], group),
+                device_id_type=MESH,
+            )
+        )
+
+        @pl.when(has[side])
+        def _():
+            early_copies[side].start()
+
     corners = corner_values(first)
     product = lex_ref[0] * spread(corners[0:1])
     for q in range(1, 8):
@@ -388,7 +409,7 @@
     pack_copies, far_copies = ([], [])
     for side in range(2):
         near, far = (4 * side, 4 - 4 * side)
-        for at, value in enumerate((nodes[near : near + 1], nodes[far : far + 1], rhs[far : far + 1], diag[far : far + 1])):
+        for at, value in enumerate((nodes[near : near + 1], nodes[far : far + 1])):
             out_pack[side, at : at + 1, :] = value
         out_far[side] = nodes[near : near + 1]
         pack_copies.append(
@@ -425,6 +446,7 @@
         @pl.when(has[side])
         def _():
             ops_copies[1 - side].wait_recv()
+            early_copies[1 - side].wait_recv()
             pack_copies[1 - side].wait_recv()
 
         @pl.when(beyond[side])
@@ -432,8 +454,8 @@
             far_copies[1 - side].wait_recv()
 
     low, high = (in_pack[0], in_pack[1])
-    far_inverse = 1.0 / jnp.where(real, planes(low[3:4], high[3:4]), 1.0)
-    far_rhs = planes(low[2:3], high[2:3])
+    far_inverse = 1.0 / jnp.where(real, planes(in_early[0][1:2], in_early[1][1:2]), 1.0)
+    far_rhs = planes(in_early[0][0:1], in_early[1][0:1])
     far_first = far_inverse * far_rhs * (1.0 / theta)
     far_remain = far_rhs - planes(low[1:2] + in_far[0], high[1:2] + in_far[1])
     remain = rhs - (nodes + planes(low[0:1], high[0:1]))
@@ -474,6 +496,7 @@
                 copy.wait_send()
             ops_copies[side].wait_send()
             pack_copies[side].wait_send()
+            early_copies[side].wait_send()
 
         @pl.when(beyond[side])
         def _():
@@ -498,8 +521,8 @@
             pltpu.VMEM((2, 2, LANES), jnp.float32),
             pltpu.VMEM((groups - 1, 2, 2, LANES), jnp.float32),
             pltpu.VMEM((2, groups, 2, LANES), jnp.float32),
-            pltpu.VMEM((2, 4, LANES), jnp.float32),
-            pltpu.VMEM((2, 4, LANES), jnp.float32),
+            pltpu.VMEM((2, 2, LANES), jnp.float32),
+            pltpu.VMEM((2, 2, LANES), jnp.float32),
             pltpu.VMEM((2, 1, LANES), jnp.float32),
             pltpu.VMEM((2, 1, LANES), jnp.float32),
             dma((groups - 1,)),
@@ -510,6 +533,10 @@
             dma((2,)),
             dma((2,)),
             dma((2,)),
+            dma((2,)),
+            dma((2,)),
+            pltpu.VMEM((2, 2, LANES), jnp.float32),
+            pltpu.VMEM((2, 2, LANES), jnp.float32),
             dma((2,)),
             dma((2,)),
         ],

time: 14.8 us -> 14.9 us (level)
  no operation moved by 1% of the time
where the time goes in v6:
time: 14.9 us; the launch traced here: 14.6 us
  Pallas kernels  14 us (94%)
  local copies, waits for them, and re-layouts  0.62 us (4%)
    pallas_call x1, Pallas kernels, one_layer(): pl.pallas_call(functools.partial(cycle_kernel, slabs, groups), out_shape=...  14 us
    unnamed x1, local copies, waits for them, and re-layouts  0.62 us

profile of v6, /device:TPU:0, one launch (start us, length us, event | category | flops | bytes accessed | tf_op | source)
XLA Modules:
  0.0 14.6 jit_solution(7433781182066942652)
XLA Ops:
  0.0 14.0 %shard_map.55 = f32[64,128]{1,0:T(8,128)S(1)} custom-call(s32[8,512]{1,0:T(8,128)} %conn_hbm.1, f32[8,8,512]{2,1,0:T(8,128)} %ops_hbm.1, f32[512,128]{1,0:T(8,128)} %res_hbm.1, f32[4,8]{1,0:T(4,128)} %bitcast.2, f32[2,4]{1,0:T(2,128)} %bitcast.3), custom_call_target="tpu_custom_call" | custom-call | tf_op jit(solution)/shard_map/pallas_call | solution.py:509
  14.0 0.6 %copy.7 = f32[64,128]{1,0:T(8,128)} copy(f32[64,128]{1,0:T(8,128)S(1)} %shard_map.55) | data formatting | bytes 65536
